TPU v7x, 32 devices: a whole 2x2x4 slice. The times are simulated.
32 devices in a mesh: groups: 2 (over y), section: 4 (over x, core), dp: 4 (over z).
Axes of the slice: x: 2, y: 2, z: 4, core: 2. Of those that a mesh axis runs over, the one named last changes fastest.
Arguments:
- patches: bfloat16 [8192, 1024], P(('groups', 'dp'), 'section'), parts along dimension 0, may hold values from -6 to 6
- clip_slot: int32 [256], P('groups'), parts along dimension 0, may hold values from 0 to 127, each once
- w_qkv: bfloat16 [4, 1024, 1536], P('section'), may hold values from -0.1875 to 0.1875
- w_out: bfloat16 [4, 512, 1024], P('section'), may hold values from -0.25 to 0.25
- w_up: bfloat16 [4, 1024, 2048], P('section'), may hold values from -0.1875 to 0.1875
- w_down: bfloat16 [4, 2048, 1024], P('section'), may hold values from -0.125 to 0.125
- norm_gains: float32 [4, 2, 1024], P('section'), may hold values from 0.5 to 1.5
- level_one_weight: bfloat16 [3, 1024, 1024], P(None, 'section'), may hold values from -0.109375 to 0.109375
- level_two_weight: bfloat16 [3, 1024, 1024], P(None, 'section'), may hold values from -0.109375 to 0.109375
- head_weight: bfloat16 [1024, 22], P('section'), may hold values from -0.1875 to 0.1875
Outputs:
- level_one_heads: float32 [256, 22], P(('groups', 'dp')), parts along dimension 0
- level_two_heads: float32 [128, 22], P(('groups', 'dp')), parts along dimension 0
There are 2 independent parts, one for each index of `groups`. A program takes and returns all parts, laid end to end along the dimension named above; an argument that names none is the same for every part. Nothing has to cross between parts.
Inputs may be any that keep to these rules, and one draw needn't show every extreme that they name: clip_slot is a permutation: every slot of the window holds exactly one clip.
All inputs are finite; a program needn't handle non-finite values.
Results may differ from a plain program's by a relative error of at most 0.035.
Values may be sent and summed in bfloat16 or wider, within the bound.
A program may use at most 64 MiB of HBM per device.

v0:
```python
import jax
import jax.numpy as jnp
from jax import lax
from jax.sharding import PartitionSpec as P

HEADS = 8
HEAD = 64
PATCHES = 16
TUB_CLIP = 2
EPSILON = 1e-05


def shifted(value, axis, steps):
    count = lax.axis_size(axis)
    leading, last = (max(0, -steps), min(count, count - steps))
    return lax.ppermute(value, axis, [(source, source + steps) for source in range(leading, last)])


def broadcast(value, axis, source):
    kept = jnp.where(lax.axis_index(axis) == source, value, 0).astype(value.dtype)
    return lax.psum(kept, axis)


def layer_norm(values, scaling):
    average = jnp.mean(values, axis=-1, keepdims=True)
    centred = values - average
    spread = jnp.mean(centred * centred, axis=-1, keepdims=True)
    return centred * lax.rsqrt(spread + EPSILON) * scaling


def head_norm(values):
    return values * lax.rsqrt(jnp.mean(values * values, axis=-1, keepdims=True) + EPSILON)


def vit_layer(stream, w_qkv, w_out, w_up, w_down, gains, clip_tok, head_count, head_size):
    row_count = stream.shape[0]
    clip_count = row_count // clip_tok
    residual = stream.astype(jnp.float32)
    normed = layer_norm(residual, gains[0]).astype(jnp.bfloat16)
    projected = jnp.dot(normed, w_qkv, preferred_element_type=jnp.float32)
    projected = projected.reshape(clip_count, clip_tok, 3, head_count, head_size)
    queries = head_norm(projected[:, :, 0]).astype(jnp.bfloat16)
    key_rows = head_norm(projected[:, :, 1]).astype(jnp.bfloat16)
    value_rows = projected[:, :, 2].astype(jnp.bfloat16)
    scores = jnp.einsum(
        "cqhd,ckhd->chqk", queries, key_rows, preferred_element_type=jnp.float32
    ) * head_size ** (-0.5)
    exponent = jnp.exp(scores)
    attention_weights = (exponent / jnp.sum(exponent, axis=-1, keepdims=True)).astype(jnp.bfloat16)
    mixture = jnp.einsum(
        "chqk,ckhd->cqhd", attention_weights, value_rows, preferred_element_type=jnp.float32
    )
    mixture = mixture.astype(jnp.bfloat16).reshape(row_count, head_count * head_size)
    residual = residual + jnp.dot(mixture, w_out, preferred_element_type=jnp.float32)
    normed_b = layer_norm(residual, gains[1]).astype(jnp.bfloat16)
    hidden = jax.nn.gelu(
        jnp.dot(normed_b, w_up, preferred_element_type=jnp.float32), approximate=True
    ).astype(jnp.bfloat16)
    residual = residual + jnp.dot(hidden, w_down, preferred_element_type=jnp.float32)
    return residual.astype(jnp.bfloat16)


def conv_terms(padded_rows, weight_local, out_rows):
    picked = [padded_rows[offset : offset + 2 * out_rows - 1 : 2] for offset in range(3)]
    stacked = jnp.concatenate(picked, axis=1)
    flat_weight = weight_local.reshape(3 * weight_local.shape[1], weight_local.shape[2])
    return jnp.dot(stacked, flat_weight, preferred_element_type=jnp.float32)


def on_device(
    patches,
    clip_slot,
    w_qkv,
    w_out,
    w_up,
    w_down,
    norm_gains,
    level_one_weight,
    level_two_weight,
    head_weight,
):
    sections = lax.axis_size("section")
    section_index = lax.axis_index("section")
    shard_index = lax.axis_index("dp")
    gathered = lax.all_gather(patches, "section", axis=1, tiled=True)
    width = gathered.shape[1]
    clip_tok = TUB_CLIP * PATCHES
    clips_dev = gathered.shape[0] // clip_tok
    per_unit = 2
    unit_rows = per_unit * clip_tok
    unit_count = clips_dev // per_unit
    tubes_unit = per_unit * TUB_CLIP
    layer_weights = (w_qkv[0], w_out[0], w_up[0], w_down[0], norm_gains[0])

    def run_layer(block_rows):
        return vit_layer(block_rows, *layer_weights, clip_tok, HEADS, HEAD)

    def pass_through(block_rows):
        return block_rows

    def advance(moment, carried):
        outgoing, pooled = carried
        arrived = shifted(outgoing, "section", 1)
        fresh_rows = lax.dynamic_slice_in_dim(
            gathered, jnp.minimum(moment, unit_count - 1) * unit_rows, unit_rows, 0
        )
        incoming = jnp.where(section_index == 0, fresh_rows, arrived)
        unit_index = moment - section_index
        active = (unit_index >= 0) & (unit_index < unit_count)
        result = lax.cond(active, run_layer, pass_through, incoming)
        tube_means = jnp.mean(
            result.astype(jnp.float32).reshape(tubes_unit, PATCHES, width), axis=1
        )
        tube_start = jnp.clip(unit_index, 0, unit_count - 1) * tubes_unit
        current = lax.dynamic_slice_in_dim(pooled, tube_start, tubes_unit, 0)
        record_here = active & (section_index == sections - 1)
        pooled = lax.dynamic_update_slice_in_dim(
            pooled, jnp.where(record_here, tube_means, current), tube_start, 0
        )
        return (result, pooled)

    empty_rows = jnp.zeros((unit_rows, width), jnp.bfloat16)
    empty_pool = jnp.zeros((clips_dev * TUB_CLIP, width), jnp.float32)
    final_rows, pooled = lax.fori_loop(
        0, unit_count + sections - 1, advance, (empty_rows, empty_pool)
    )
    pooled = broadcast(pooled.astype(jnp.bfloat16), "section", sections - 1)
    local_positions = pooled.shape[0]
    film_position = (
        clip_slot[:, None] * TUB_CLIP + jnp.arange(TUB_CLIP, dtype=jnp.int32)[None, :]
    ).reshape(-1)
    targets = shard_index * local_positions + jnp.arange(local_positions, dtype=jnp.int32)
    selector = (targets[:, None] == film_position[None, :]).astype(jnp.bfloat16)
    film_rows = jnp.dot(
        selector,
        lax.all_gather(pooled, "dp", axis=0, tiled=True),
        preferred_element_type=jnp.float32,
    )
    film_rows = film_rows.astype(jnp.bfloat16)
    channels = width // sections
    chan_start = section_index * channels
    input_share = lax.dynamic_slice_in_dim(film_rows, chan_start, channels, 1)
    level_one_rows = local_positions // 2
    edge_input = shifted(input_share[-3:], "dp", 1)
    one_rows = level_one_rows + 1
    padded_input = jnp.concatenate([edge_input, input_share], axis=0)
    one_partial = conv_terms(padded_input, level_one_weight, one_rows)
    one_total = lax.psum(one_partial.astype(jnp.bfloat16), "section").astype(jnp.float32)
    one_total = lax.dynamic_slice_in_dim(one_total, chan_start, channels, 1)
    one_share = jax.nn.gelu(one_total, approximate=True).astype(jnp.bfloat16)
    level_one_out = one_share[1:]
    two_partial = conv_terms(one_share, level_two_weight, level_one_rows // 2)
    two_total = lax.psum(two_partial.astype(jnp.bfloat16), "section").astype(jnp.float32)
    two_total = lax.dynamic_slice_in_dim(two_total, chan_start, channels, 1)
    two_share = jax.nn.gelu(two_total, approximate=True).astype(jnp.bfloat16)
    head_one = jnp.dot(level_one_out, head_weight, preferred_element_type=jnp.float32)
    head_two = jnp.dot(two_share, head_weight, preferred_element_type=jnp.float32)
    head_one, head_two = lax.psum((head_one, head_two), "section")
    return (head_one, head_two)


def solution(mesh):
    return jax.shard_map(
        on_device,
        mesh=mesh,
        in_specs=(
            P(("groups", "dp"), "section"),
            P("groups"),
            P("section", None, None),
            P("section", None, None),
            P("section", None, None),
            P("section", None, None),
            P("section", None, None),
            P(None, "section", None),
            P(None, "section", None),
            P("section", None),
        ),
        out_specs=(P(("groups", "dp"), None), P(("groups", "dp"), None)),
        check_vma=False,
    )
```

profile of v0, /device:TPU:0, one launch (start us, length us, event | category | flops | bytes accessed | tf_op | source)
XLA Modules:
  0.0 553.1 jit_solution(6364947643892078391)
XLA Ops:
  9.4 25.7 %all-gather.2.cloned.1.call-done = bf16[1024,1024]{1,0:T(8,128)(2,1)} async-done(((bf16[1024,256]{1,0:T(8,128)(2,1)}), bf16[1024,1024]{1,0:T(8,128)(2,1)}) %all-gather.2.cloned.1.call-update) | async-done | bytes 2097168 | tf_op jit(solution)/shard_map/all_gather | solution.py:85
  35.8 372.3 %while.16 = (s32[]{:T(128)}, bf16[64,1024]{1,0:T(8,128)(2,1)S(1)}, bf16[64,1024]{1,0:T(8,128)(2,1)}, s32[]{:T(128)}, pred[]{:T(512)}, /*index=5*/bf16[1024,1024]...) while((s32[]{:T(128)}, bf16[64,1024]{1,0:T(8,128)(2,1)S(1)}, ...), condition=%wide.region_12.13_spmd, body=%wide.region_0.12_spmd.sunk | while | flops 812734080 | bytes 22180840 | solution.py:124
  39.9 13.1 %conditional.2 = (bf16[64,1024]{1,0:T(8,128)(2,1)S(1)}, f32[4,1024]{1,0:T(4,128)S(1)}) conditional(s32[]{:T(128)} %convert_element_type.183, bf16[64,1024]{1,0:T(8,128)(2,1)S(1)} %dynamic-slice_select_fusion.2, (bf16[64,1024]{1,0:T(8,128)(2,1)S(1)}, f32[2,1024]{1,0:T(2,128)}, bf16[1024,1536]{1,0:T(8,128)(2,1)}, bf16[512,1024]{1,0:T(8,128)(2,1)}, ...), branch_computations={%region_1.0_spmd, %region_3.11_spmd} | conditional | flops 812660352 | bytes 21230124 | solution.py:110
  47.7 5.3 convert_reduce_fusion.2
  57.5 13.1 %conditional.2 = (bf16[64,1024]{1,0:T(8,128)(2,1)S(1)}, f32[4,1024]{1,0:T(4,128)S(1)}) conditional(s32[]{:T(128)} %convert_element_type.183, bf16[64,1024]{1,0:T(8,128)(2,1)S(1)} %dynamic-slice_select_fusion.2, (bf16[64,1024]{1,0:T(8,128)(2,1)S(1)}, f32[2,1024]{1,0:T(2,128)}, bf16[1024,1536]{1,0:T(8,128)(2,1)}, bf16[512,1024]{1,0:T(8,128)(2,1)}, ...), branch_computations={%region_1.0_spmd, %region_3.11_spmd} | conditional | flops 812660352 | bytes 21230124 | solution.py:110
  65.3 5.3 convert_reduce_fusion.2
  76.1 13.1 %conditional.2 = (bf16[64,1024]{1,0:T(8,128)(2,1)S(1)}, f32[4,1024]{1,0:T(4,128)S(1)}) conditional(s32[]{:T(128)} %convert_element_type.183, bf16[64,1024]{1,0:T(8,128)(2,1)S(1)} %dynamic-slice_select_fusion.2, (bf16[64,1024]{1,0:T(8,128)(2,1)S(1)}, f32[2,1024]{1,0:T(2,128)}, bf16[1024,1536]{1,0:T(8,128)(2,1)}, bf16[512,1024]{1,0:T(8,128)(2,1)}, ...), branch_computations={%region_1.0_spmd, %region_3.11_spmd} | conditional | flops 812660352 | bytes 21230124 | solution.py:110
  83.9 5.3 convert_reduce_fusion.2
  95.2 13.1 %conditional.2 = (bf16[64,1024]{1,0:T(8,128)(2,1)S(1)}, f32[4,1024]{1,0:T(4,128)S(1)}) conditional(s32[]{:T(128)} %convert_element_type.183, bf16[64,1024]{1,0:T(8,128)(2,1)S(1)} %dynamic-slice_select_fusion.2, (bf16[64,1024]{1,0:T(8,128)(2,1)S(1)}, f32[2,1024]{1,0:T(2,128)}, bf16[1024,1536]{1,0:T(8,128)(2,1)}, bf16[512,1024]{1,0:T(8,128)(2,1)}, ...), branch_computations={%region_1.0_spmd, %region_3.11_spmd} | conditional | flops 812660352 | bytes 21230124 | solution.py:110
  103.0 5.3 convert_reduce_fusion.2
  109.7 5.3 collective-permute-start
  116.9 13.1 %conditional.2 = (bf16[64,1024]{1,0:T(8,128)(2,1)S(1)}, f32[4,1024]{1,0:T(4,128)S(1)}) conditional(s32[]{:T(128)} %convert_element_type.183, bf16[64,1024]{1,0:T(8,128)(2,1)S(1)} %dynamic-slice_select_fusion.2, (bf16[64,1024]{1,0:T(8,128)(2,1)S(1)}, f32[2,1024]{1,0:T(2,128)}, bf16[1024,1536]{1,0:T(8,128)(2,1)}, bf16[512,1024]{1,0:T(8,128)(2,1)}, ...), branch_computations={%region_1.0_spmd, %region_3.11_spmd} | conditional | flops 812660352 | bytes 21230124 | solution.py:110
  124.7 5.3 convert_reduce_fusion.2
  131.3 5.3 collective-permute-start
  138.5 13.1 %conditional.2 = (bf16[64,1024]{1,0:T(8,128)(2,1)S(1)}, f32[4,1024]{1,0:T(4,128)S(1)}) conditional(s32[]{:T(128)} %convert_element_type.183, bf16[64,1024]{1,0:T(8,128)(2,1)S(1)} %dynamic-slice_select_fusion.2, (bf16[64,1024]{1,0:T(8,128)(2,1)S(1)}, f32[2,1024]{1,0:T(2,128)}, bf16[1024,1536]{1,0:T(8,128)(2,1)}, bf16[512,1024]{1,0:T(8,128)(2,1)}, ...), branch_computations={%region_1.0_spmd, %region_3.11_spmd} | conditional | flops 812660352 | bytes 21230124 | solution.py:110
  152.9 5.3 collective-permute-start
  160.1 13.1 %conditional.2 = (bf16[64,1024]{1,0:T(8,128)(2,1)S(1)}, f32[4,1024]{1,0:T(4,128)S(1)}) conditional(s32[]{:T(128)} %convert_element_type.183, bf16[64,1024]{1,0:T(8,128)(2,1)S(1)} %dynamic-slice_select_fusion.2, (bf16[64,1024]{1,0:T(8,128)(2,1)S(1)}, f32[2,1024]{1,0:T(2,128)}, bf16[1024,1536]{1,0:T(8,128)(2,1)}, bf16[512,1024]{1,0:T(8,128)(2,1)}, ...), branch_computations={%region_1.0_spmd, %region_3.11_spmd} | conditional | flops 812660352 | bytes 21230124 | solution.py:110
  167.9 5.3 convert_reduce_fusion.2
  174.5 5.3 collective-permute-start
  181.8 13.1 %conditional.2 = (bf16[64,1024]{1,0:T(8,128)(2,1)S(1)}, f32[4,1024]{1,0:T(4,128)S(1)}) conditional(s32[]{:T(128)} %convert_element_type.183, bf16[64,1024]{1,0:T(8,128)(2,1)S(1)} %dynamic-slice_select_fusion.2, (bf16[64,1024]{1,0:T(8,128)(2,1)S(1)}, f32[2,1024]{1,0:T(2,128)}, bf16[1024,1536]{1,0:T(8,128)(2,1)}, bf16[512,1024]{1,0:T(8,128)(2,1)}, ...), branch_computations={%region_1.0_spmd, %region_3.11_spmd} | conditional | flops 812660352 | bytes 21230124 | solution.py:110
  196.2 5.3 collective-permute-start
  203.4 13.1 %conditional.2 = (bf16[64,1024]{1,0:T(8,128)(2,1)S(1)}, f32[4,1024]{1,0:T(4,128)S(1)}) conditional(s32[]{:T(128)} %convert_element_type.183, bf16[64,1024]{1,0:T(8,128)(2,1)S(1)} %dynamic-slice_select_fusion.2, (bf16[64,1024]{1,0:T(8,128)(2,1)S(1)}, f32[2,1024]{1,0:T(2,128)}, bf16[1024,1536]{1,0:T(8,128)(2,1)}, bf16[512,1024]{1,0:T(8,128)(2,1)}, ...), branch_computations={%region_1.0_spmd, %region_3.11_spmd} | conditional | flops 812660352 | bytes 21230124 | solution.py:110
  211.2 5.3 convert_reduce_fusion.2
  217.8 5.3 collective-permute-start
  225.0 13.1 %conditional.2 = (bf16[64,1024]{1,0:T(8,128)(2,1)S(1)}, f32[4,1024]{1,0:T(4,128)S(1)}) conditional(s32[]{:T(128)} %convert_element_type.183, bf16[64,1024]{1,0:T(8,128)(2,1)S(1)} %dynamic-slice_select_fusion.2, (bf16[64,1024]{1,0:T(8,128)(2,1)S(1)}, f32[2,1024]{1,0:T(2,128)}, bf16[1024,1536]{1,0:T(8,128)(2,1)}, bf16[512,1024]{1,0:T(8,128)(2,1)}, ...), branch_computations={%region_1.0_spmd, %region_3.11_spmd} | conditional | flops 812660352 | bytes 21230124 | solution.py:110
  232.8 5.3 convert_reduce_fusion.2
  239.4 5.3 collective-permute-start
  246.6 13.1 %conditional.2 = (bf16[64,1024]{1,0:T(8,128)(2,1)S(1)}, f32[4,1024]{1,0:T(4,128)S(1)}) conditional(s32[]{:T(128)} %convert_element_type.183, bf16[64,1024]{1,0:T(8,128)(2,1)S(1)} %dynamic-slice_select_fusion.2, (bf16[64,1024]{1,0:T(8,128)(2,1)S(1)}, f32[2,1024]{1,0:T(2,128)}, bf16[1024,1536]{1,0:T(8,128)(2,1)}, bf16[512,1024]{1,0:T(8,128)(2,1)}, ...), branch_computations={%region_1.0_spmd, %region_3.11_spmd} | conditional | flops 812660352 | bytes 21230124 | solution.py:110
  254.4 5.3 convert_reduce_fusion.2
  261.0 5.3 collective-permute-start
  268.3 13.1 %conditional.2 = (bf16[64,1024]{1,0:T(8,128)(2,1)S(1)}, f32[4,1024]{1,0:T(4,128)S(1)}) conditional(s32[]{:T(128)} %convert_element_type.183, bf16[64,1024]{1,0:T(8,128)(2,1)S(1)} %dynamic-slice_select_fusion.2, (bf16[64,1024]{1,0:T(8,128)(2,1)S(1)}, f32[2,1024]{1,0:T(2,128)}, bf16[1024,1536]{1,0:T(8,128)(2,1)}, bf16[512,1024]{1,0:T(8,128)(2,1)}, ...), branch_computations={%region_1.0_spmd, %region_3.11_spmd} | conditional | flops 812660352 | bytes 21230124 | solution.py:110
  276.1 5.3 convert_reduce_fusion.2
  282.7 5.3 collective-permute-start
  289.9 13.1 %conditional.2 = (bf16[64,1024]{1,0:T(8,128)(2,1)S(1)}, f32[4,1024]{1,0:T(4,128)S(1)}) conditional(s32[]{:T(128)} %convert_element_type.183, bf16[64,1024]{1,0:T(8,128)(2,1)S(1)} %dynamic-slice_select_fusion.2, (bf16[64,1024]{1,0:T(8,128)(2,1)S(1)}, f32[2,1024]{1,0:T(2,128)}, bf16[1024,1536]{1,0:T(8,128)(2,1)}, bf16[512,1024]{1,0:T(8,128)(2,1)}, ...), branch_computations={%region_1.0_spmd, %region_3.11_spmd} | conditional | flops 812660352 | bytes 21230124 | solution.py:110
  304.3 5.3 collective-permute-start
  311.5 13.1 %conditional.2 = (bf16[64,1024]{1,0:T(8,128)(2,1)S(1)}, f32[4,1024]{1,0:T(4,128)S(1)}) conditional(s32[]{:T(128)} %convert_element_type.183, bf16[64,1024]{1,0:T(8,128)(2,1)S(1)} %dynamic-slice_select_fusion.2, (bf16[64,1024]{1,0:T(8,128)(2,1)S(1)}, f32[2,1024]{1,0:T(2,128)}, bf16[1024,1536]{1,0:T(8,128)(2,1)}, bf16[512,1024]{1,0:T(8,128)(2,1)}, ...), branch_computations={%region_1.0_spmd, %region_3.11_spmd} | conditional | flops 812660352 | bytes 21230124 | solution.py:110
  325.9 5.3 collective-permute-start
  333.1 13.1 %conditional.2 = (bf16[64,1024]{1,0:T(8,128)(2,1)S(1)}, f32[4,1024]{1,0:T(4,128)S(1)}) conditional(s32[]{:T(128)} %convert_element_type.183, bf16[64,1024]{1,0:T(8,128)(2,1)S(1)} %dynamic-slice_select_fusion.2, (bf16[64,1024]{1,0:T(8,128)(2,1)S(1)}, f32[2,1024]{1,0:T(2,128)}, bf16[1024,1536]{1,0:T(8,128)(2,1)}, bf16[512,1024]{1,0:T(8,128)(2,1)}, ...), branch_computations={%region_1.0_spmd, %region_3.11_spmd} | conditional | flops 812660352 | bytes 21230124 | solution.py:110
  347.5 5.3 collective-permute-start
  354.8 13.1 %conditional.2 = (bf16[64,1024]{1,0:T(8,128)(2,1)S(1)}, f32[4,1024]{1,0:T(4,128)S(1)}) conditional(s32[]{:T(128)} %convert_element_type.183, bf16[64,1024]{1,0:T(8,128)(2,1)S(1)} %dynamic-slice_select_fusion.2, (bf16[64,1024]{1,0:T(8,128)(2,1)S(1)}, f32[2,1024]{1,0:T(2,128)}, bf16[1024,1536]{1,0:T(8,128)(2,1)}, bf16[512,1024]{1,0:T(8,128)(2,1)}, ...), branch_computations={%region_1.0_spmd, %region_3.11_spmd} | conditional | flops 812660352 | bytes 21230124 | solution.py:110
  369.2 5.3 collective-permute-start
  377.8 18.3 %collective-permute-start = (bf16[64,1024]{1,0:T(8,128)(2,1)S(1)}, bf16[64,1024]{1,0:T(8,128)(2,1)S(1)}, u32[]{:S(2)}, u32[]{:S(2)}) collective-permute-start(bf16[64,1024]{1,0:T(8,128)(2,1)S(1)} %get-tuple-element.386), channel_id=1, source_target_pairs={{0,4},{4,8},{8,12},{1,5},{5,9},{9,13},{2,6},{6,10},{10,14},{3,7},{... | collective-permute-start | bytes 393224 | tf_op jit(solution)/shard_map/while/body/eval_jaxpr/ppermute | solution.py:16
  399.4 5.3 collective-permute-start
  408.8 60.7 %all-reduce.4.cloned.1.call-done = bf16[64,1024]{1,0:T(8,128)(2,1)} async-done(((bf16[64,1024]{1,0:T(8,128)(2,1)}), bf16[64,1024]{1,0:T(8,128)(2,1)}) %all-reduce.4.cloned.1.call-update) | async-done | bytes 131088 | tf_op jit(solution)/shard_map/psum | solution.py:21
  469.5 14.9 %all_gather.7 = bf16[256,1024]{1,0:T(8,128)(2,1)S(1)} all-gather(bf16[64,1024]{1,0:T(8,128)(2,1)} %all-reduce.4.cloned.1.call-done), channel_id=1, replica_groups=mesh['groups'=2,'section'=4,'dp'=4] {'dp'}, dimensions={0}, use_global_device_ids=true | all-gather | bytes 655360 | tf_op jit(solution)/shard_map/all_gather | solution.py:136
  491.8 31.6 %all-reduce.6.cloned.1.call-done = bf16[33,1024]{1,0:T(8,128)(2,1)} async-done(((bf16[33,1024]{1,0:T(8,128)(2,1)}), bf16[33,1024]{1,0:T(8,128)(2,1)}) %all-reduce.6.cloned.1.call-update) | async-done | bytes 67600 | tf_op jit(solution)/shard_map/psum | solution.py:148
  524.6 10.7 %psum.38 = bf16[16,1024]{1,0:T(8,128)(2,1)S(1)} all-reduce(bf16[16,1024]{1,0:T(8,128)(2,1)S(1)} %convolution_convert_fusion.2), channel_id=1, replica_groups=mesh['groups'=2,'section'=4,'dp'=4] {'section'}, use_global_device_ids=true, to_apply=%region_16.17 | all-reduce | flops 16384 | bytes 65536 | tf_op jit(solution)/shard_map/psum | solution.py:153
  535.4 11.1 %all-reduce = (f32[32,22]{0,1:T(8,128)}, f32[16,22]{1,0:T(8,128)}) all-reduce(f32[32,22]{0,1:T(8,128)S(1)} %fusion.70, f32[16,22]{1,0:T(8,128)S(1)} %fusion.72), channel_id=1, replica_groups=mesh['groups'=2,'section'=4,'dp'=4] {'section'}, use_global_device_ids=true, to_apply=%region_15.16 | all-reduce | flops 1056 | bytes 8448 | tf_op jit(solution)/shard_map/psum | solution.py:158
  (461 shorter events, 236.8 us)
Async XLA Ops:
  7.2 483.6 %copy-start = (bf16[3,256,1024]{2,1,0:T(8,128)(2,1)S(1)}, bf16[3,256,1024]{2,1,0:T(8,128)(2,1)}, u32[]{:S(2)}) copy-start(bf16[3,256,1024]{2,1,0:T(8,128)(2,1)} %param.21) | copy-start | bytes 4718596
  7.2 27.9 %all-gather.2.cloned.1.call-start = ((), (), s32[]{:S(2)}) async-start(), calls=%async_computation | async-start | bytes 2621440 | tf_op jit(solution)/shard_map/all_gather | solution.py:85
  7.9 461.6 %all-reduce.4.cloned.1.call-start = ((), (), s32[]{:S(2)}) async-start(), calls=%async_computation.1 | async-start | bytes 262144 | tf_op jit(solution)/shard_map/psum | solution.py:21
  35.8 3.1 collective-permute-start
  44.4 2.7 copy-start.1
  54.3 2.3 collective-permute-start
  62.0 2.7 copy-start.1
  71.9 3.2 collective-permute-start
  80.6 2.7 copy-start.1
  90.5 3.8 collective-permute-start
  99.8 2.7 copy-start.1
  109.7 6.3 %collective-permute-start = (bf16[64,1024]{1,0:T(8,128)(2,1)S(1)}, bf16[64,1024]{1,0:T(8,128)(2,1)S(1)}, u32[]{:S(2)}, u32[]{:S(2)}) collective-permute-start(bf16[64,1024]{1,0:T(8,128)(2,1)S(1)} %get-tuple-element.386), channel_id=1, source_target_pairs={{0,4},{4,8},{8,12},{1,5},{5,9},{9,13},{2,6},{6,10},{10,14},{3,7},{... | collective-permute-start | bytes 393224 | tf_op jit(solution)/shard_map/while/body/eval_jaxpr/ppermute | solution.py:16
  121.4 2.7 copy-start.1
  131.3 6.3 %collective-permute-start = (bf16[64,1024]{1,0:T(8,128)(2,1)S(1)}, bf16[64,1024]{1,0:T(8,128)(2,1)S(1)}, u32[]{:S(2)}, u32[]{:S(2)}) collective-permute-start(bf16[64,1024]{1,0:T(8,128)(2,1)S(1)} %get-tuple-element.386), channel_id=1, source_target_pairs={{0,4},{4,8},{8,12},{1,5},{5,9},{9,13},{2,6},{6,10},{10,14},{3,7},{... | collective-permute-start | bytes 393224 | tf_op jit(solution)/shard_map/while/body/eval_jaxpr/ppermute | solution.py:16
  143.0 2.7 copy-start.1
  152.9 6.3 %collective-permute-start = (bf16[64,1024]{1,0:T(8,128)(2,1)S(1)}, bf16[64,1024]{1,0:T(8,128)(2,1)S(1)}, u32[]{:S(2)}, u32[]{:S(2)}) collective-permute-start(bf16[64,1024]{1,0:T(8,128)(2,1)S(1)} %get-tuple-element.386), channel_id=1, source_target_pairs={{0,4},{4,8},{8,12},{1,5},{5,9},{9,13},{2,6},{6,10},{10,14},{3,7},{... | collective-permute-start | bytes 393224 | tf_op jit(solution)/shard_map/while/body/eval_jaxpr/ppermute | solution.py:16
  164.6 2.7 copy-start.1
  174.5 6.3 %collective-permute-start = (bf16[64,1024]{1,0:T(8,128)(2,1)S(1)}, bf16[64,1024]{1,0:T(8,128)(2,1)S(1)}, u32[]{:S(2)}, u32[]{:S(2)}) collective-permute-start(bf16[64,1024]{1,0:T(8,128)(2,1)S(1)} %get-tuple-element.386), channel_id=1, source_target_pairs={{0,4},{4,8},{8,12},{1,5},{5,9},{9,13},{2,6},{6,10},{10,14},{3,7},{... | collective-permute-start | bytes 393224 | tf_op jit(solution)/shard_map/while/body/eval_jaxpr/ppermute | solution.py:16
  186.3 2.7 copy-start.1
  196.2 6.3 %collective-permute-start = (bf16[64,1024]{1,0:T(8,128)(2,1)S(1)}, bf16[64,1024]{1,0:T(8,128)(2,1)S(1)}, u32[]{:S(2)}, u32[]{:S(2)}) collective-permute-start(bf16[64,1024]{1,0:T(8,128)(2,1)S(1)} %get-tuple-element.386), channel_id=1, source_target_pairs={{0,4},{4,8},{8,12},{1,5},{5,9},{9,13},{2,6},{6,10},{10,14},{3,7},{... | collective-permute-start | bytes 393224 | tf_op jit(solution)/shard_map/while/body/eval_jaxpr/ppermute | solution.py:16
  207.9 2.7 copy-start.1
  217.8 6.3 %collective-permute-start = (bf16[64,1024]{1,0:T(8,128)(2,1)S(1)}, bf16[64,1024]{1,0:T(8,128)(2,1)S(1)}, u32[]{:S(2)}, u32[]{:S(2)}) collective-permute-start(bf16[64,1024]{1,0:T(8,128)(2,1)S(1)} %get-tuple-element.386), channel_id=1, source_target_pairs={{0,4},{4,8},{8,12},{1,5},{5,9},{9,13},{2,6},{6,10},{10,14},{3,7},{... | collective-permute-start | bytes 393224 | tf_op jit(solution)/shard_map/while/body/eval_jaxpr/ppermute | solution.py:16
  229.5 2.7 copy-start.1
  239.4 6.3 %collective-permute-start = (bf16[64,1024]{1,0:T(8,128)(2,1)S(1)}, bf16[64,1024]{1,0:T(8,128)(2,1)S(1)}, u32[]{:S(2)}, u32[]{:S(2)}) collective-permute-start(bf16[64,1024]{1,0:T(8,128)(2,1)S(1)} %get-tuple-element.386), channel_id=1, source_target_pairs={{0,4},{4,8},{8,12},{1,5},{5,9},{9,13},{2,6},{6,10},{10,14},{3,7},{... | collective-permute-start | bytes 393224 | tf_op jit(solution)/shard_map/while/body/eval_jaxpr/ppermute | solution.py:16
  251.2 2.7 copy-start.1
  261.0 6.3 %collective-permute-start = (bf16[64,1024]{1,0:T(8,128)(2,1)S(1)}, bf16[64,1024]{1,0:T(8,128)(2,1)S(1)}, u32[]{:S(2)}, u32[]{:S(2)}) collective-permute-start(bf16[64,1024]{1,0:T(8,128)(2,1)S(1)} %get-tuple-element.386), channel_id=1, source_target_pairs={{0,4},{4,8},{8,12},{1,5},{5,9},{9,13},{2,6},{6,10},{10,14},{3,7},{... | collective-permute-start | bytes 393224 | tf_op jit(solution)/shard_map/while/body/eval_jaxpr/ppermute | solution.py:16
  272.8 2.7 copy-start.1
  282.7 6.3 %collective-permute-start = (bf16[64,1024]{1,0:T(8,128)(2,1)S(1)}, bf16[64,1024]{1,0:T(8,128)(2,1)S(1)}, u32[]{:S(2)}, u32[]{:S(2)}) collective-permute-start(bf16[64,1024]{1,0:T(8,128)(2,1)S(1)} %get-tuple-element.386), channel_id=1, source_target_pairs={{0,4},{4,8},{8,12},{1,5},{5,9},{9,13},{2,6},{6,10},{10,14},{3,7},{... | collective-permute-start | bytes 393224 | tf_op jit(solution)/shard_map/while/body/eval_jaxpr/ppermute | solution.py:16
  294.4 2.7 copy-start.1
  304.3 6.3 %collective-permute-start = (bf16[64,1024]{1,0:T(8,128)(2,1)S(1)}, bf16[64,1024]{1,0:T(8,128)(2,1)S(1)}, u32[]{:S(2)}, u32[]{:S(2)}) collective-permute-start(bf16[64,1024]{1,0:T(8,128)(2,1)S(1)} %get-tuple-element.386), channel_id=1, source_target_pairs={{0,4},{4,8},{8,12},{1,5},{5,9},{9,13},{2,6},{6,10},{10,14},{3,7},{... | collective-permute-start | bytes 393224 | tf_op jit(solution)/shard_map/while/body/eval_jaxpr/ppermute | solution.py:16
  316.0 2.7 copy-start.1
  325.9 6.3 %collective-permute-start = (bf16[64,1024]{1,0:T(8,128)(2,1)S(1)}, bf16[64,1024]{1,0:T(8,128)(2,1)S(1)}, u32[]{:S(2)}, u32[]{:S(2)}) collective-permute-start(bf16[64,1024]{1,0:T(8,128)(2,1)S(1)} %get-tuple-element.386), channel_id=1, source_target_pairs={{0,4},{4,8},{8,12},{1,5},{5,9},{9,13},{2,6},{6,10},{10,14},{3,7},{... | collective-permute-start | bytes 393224 | tf_op jit(solution)/shard_map/while/body/eval_jaxpr/ppermute | solution.py:16
  337.7 2.7 copy-start.1
  347.5 6.3 %collective-permute-start = (bf16[64,1024]{1,0:T(8,128)(2,1)S(1)}, bf16[64,1024]{1,0:T(8,128)(2,1)S(1)}, u32[]{:S(2)}, u32[]{:S(2)}) collective-permute-start(bf16[64,1024]{1,0:T(8,128)(2,1)S(1)} %get-tuple-element.386), channel_id=1, source_target_pairs={{0,4},{4,8},{8,12},{1,5},{5,9},{9,13},{2,6},{6,10},{10,14},{3,7},{... | collective-permute-start | bytes 393224 | tf_op jit(solution)/shard_map/while/body/eval_jaxpr/ppermute | solution.py:16
  359.3 2.7 copy-start.1
  369.2 6.3 %collective-permute-start = (bf16[64,1024]{1,0:T(8,128)(2,1)S(1)}, bf16[64,1024]{1,0:T(8,128)(2,1)S(1)}, u32[]{:S(2)}, u32[]{:S(2)}) collective-permute-start(bf16[64,1024]{1,0:T(8,128)(2,1)S(1)} %get-tuple-element.386), channel_id=1, source_target_pairs={{0,4},{4,8},{8,12},{1,5},{5,9},{9,13},{2,6},{6,10},{10,14},{3,7},{... | collective-permute-start | bytes 393224 | tf_op jit(solution)/shard_map/while/body/eval_jaxpr/ppermute | solution.py:16
  377.8 19.3 %collective-permute-start = (bf16[64,1024]{1,0:T(8,128)(2,1)S(1)}, bf16[64,1024]{1,0:T(8,128)(2,1)S(1)}, u32[]{:S(2)}, u32[]{:S(2)}) collective-permute-start(bf16[64,1024]{1,0:T(8,128)(2,1)S(1)} %get-tuple-element.386), channel_id=1, source_target_pairs={{0,4},{4,8},{8,12},{1,5},{5,9},{9,13},{2,6},{6,10},{10,14},{3,7},{... | collective-permute-start | bytes 393224 | tf_op jit(solution)/shard_map/while/body/eval_jaxpr/ppermute | solution.py:16
  399.4 6.3 %collective-permute-start = (bf16[64,1024]{1,0:T(8,128)(2,1)S(1)}, bf16[64,1024]{1,0:T(8,128)(2,1)S(1)}, u32[]{:S(2)}, u32[]{:S(2)}) collective-permute-start(bf16[64,1024]{1,0:T(8,128)(2,1)S(1)} %get-tuple-element.386), channel_id=1, source_target_pairs={{0,4},{4,8},{8,12},{1,5},{5,9},{9,13},{2,6},{6,10},{10,14},{3,7},{... | collective-permute-start | bytes 393224 | tf_op jit(solution)/shard_map/while/body/eval_jaxpr/ppermute | solution.py:16
  408.0 116.1 %copy-start.3 = (bf16[256,22]{0,1:T(8,128)(2,1)S(1)}, bf16[256,22]{0,1:T(8,128)(2,1)}, u32[]{:S(2)}) copy-start(bf16[256,22]{0,1:T(8,128)(2,1)} %param.23) | copy-start | bytes 33796
  408.0 116.2 %copy-start.2 = (bf16[3,256,1024]{2,1,0:T(8,128)(2,1)S(1)}, bf16[3,256,1024]{2,1,0:T(8,128)(2,1)}, u32[]{:S(2)}) copy-start(bf16[3,256,1024]{2,1,0:T(8,128)(2,1)} %param.22) | copy-start | bytes 4718596
  408.7 114.6 %all-reduce.6.cloned.1.call-start = ((), (), s32[]{:S(2)}) async-start(), calls=%async_computation.2 | async-start | bytes 163840 | tf_op jit(solution)/shard_map/psum | solution.py:148
  485.3 5.3 collective-permute-start.1
Sparse Core Ops, SparseCore 0:
  9.5 25.5 all-gather.1
  408.8 60.5 all-reduce.3
  491.9 31.3 all-reduce.5
where the time goes:
time: 557 us; the launch traced here: 553 us
  matrix products  158 us (28%)
  waiting for transfers between devices  138 us (25%)
  starting transfers between devices  105 us (19%)
  other arithmetic  57.8 us (10%)
  local copies, waits for them, and re-layouts  41 us (7%)
  blocking collectives  36.7 us (7%)
  between operations  13.9 us (2%)
    ppermute x20, starting transfers between devices, shifted(): lax.ppermute(value, axis, [(source, source + steps) for source in range(l...  105 us
    dot_general x16, matrix products, vit_layer(): jnp.dot(hidden, w_down, preferred_element_type=jnp.float32)  84.4 us
    psum x1, waiting for transfers between devices, broadcast(): return lax.psum(kept, axis)  60.7 us
    dot_general x16, matrix products, vit_layer(): projected = jnp.dot(normed, w_qkv, preferred_element_type=jnp.float32)  41.3 us
    psum x1, waiting for transfers between devices, on_device(): lax.psum(one_partial.astype(jnp.bfloat16), 'section').astype(jnp.float32)  31.6 us
    all_gather x1, waiting for transfers between devices, on_device(): gathered = lax.all_gather(patches, 'section', axis=1, tiled=True)  25.7 us
    dynamic_update_slice x19, other arithmetic, advance(): lax.dynamic_update_slice_in_dim(pooled, jnp.where(record_here, tube_means...  25.3 us
    slice x16, local copies, waits for them, and re-layouts, vit_layer(): normed_b = layer_norm(residual, gains[1]).astype(jnp.bfloat16)  22.1 us
  transfers between devices with their start and end apart: 23, of which 23 were waited for; matrix products, arithmetic and copies ran while one was open for 0% of the time, Pallas kernels for 0%

commit v1 on v0

--- a/solution.py
+++ b/solution.py
@@ -18,7 +18,7 @@
 
 def broadcast(value, axis, source):
     kept = jnp.where(lax.axis_index(axis) == source, value, 0).astype(value.dtype)
-    return lax.psum(kept, axis)
+    return jnp.sum(lax.all_gather(kept, axis), axis=0)
 
 
 def layer_norm(values, scaling):

time: 557 us -> 532 us (0.955)
  waiting for transfers between devices: 138 us -> 76.2 us
  blocking collectives: 36.7 us -> 72.8 us
    psum x1 -> x0, waiting for transfers between devices: 60.7 us -> none  [broadcast(): return lax.psum(kept, axis)]
    all_gather x0 -> x1, blocking collectives: none -> 34.8 us  [broadcast(): return jnp.sum(lax.all_gather(kept, axis), axis=0)]
  transfers between devices with their start and end apart: 23 -> 22, of which waited for: 23 -> 22; matrix products, arithmetic and copies ran while one was open for 0% -> 0% of each run, Pallas kernels for 0% -> 0%
where the time goes in v1:
time: 532 us; the launch traced here: 528 us
  matrix products  158 us (30%)
  starting transfers between devices  105 us (20%)
  waiting for transfers between devices  76.2 us (14%)
  blocking collectives  72.8 us (14%)
  other arithmetic  57.8 us (11%)
  local copies, waits for them, and re-layouts  41 us (8%)
  between operations  14.2 us (3%)
    ppermute x20, starting transfers between devices, shifted(): lax.ppermute(value, axis, [(source, source + steps) for source in range(l...  105 us
    dot_general x16, matrix products, vit_layer(): jnp.dot(hidden, w_down, preferred_element_type=jnp.float32)  84.4 us
    dot_general x16, matrix products, vit_layer(): projected = jnp.dot(normed, w_qkv, preferred_element_type=jnp.float32)  41.3 us
    all_gather x1, blocking collectives, broadcast(): return jnp.sum(lax.all_gather(kept, axis), axis=0)  34.8 us
    psum x1, waiting for transfers between devices, on_device(): lax.psum(one_partial.astype(jnp.bfloat16), 'section').astype(jnp.float32)  31.3 us
    dynamic_update_slice x19, other arithmetic, advance(): lax.dynamic_update_slice_in_dim(pooled, jnp.where(record_here, tube_means...  25.3 us
    all_gather x1, waiting for transfers between devices, on_device(): gathered = lax.all_gather(patches, 'section', axis=1, tiled=True)  25.2 us
    slice x16, local copies, waits for them, and re-layouts, vit_layer(): normed_b = layer_norm(residual, gains[1]).astype(jnp.bfloat16)  22.1 us
  transfers between devices with their start and end apart: 22, of which 22 were waited for; matrix products, arithmetic and copies ran while one was open for 0% of the time, Pallas kernels for 0%

profile of v1, /device:TPU:0, one launch (start us, length us, event | category | flops | bytes accessed | tf_op | source)
XLA Modules:
  0.0 527.7 jit_solution(18295115380564435925)
XLA Ops:
  9.9 25.2 %all-gather.3.cloned.1.call-done = bf16[1024,1024]{1,0:T(8,128)(2,1)} async-done(((bf16[1024,256]{1,0:T(8,128)(2,1)}), bf16[1024,1024]{1,0:T(8,128)(2,1)}) %all-gather.3.cloned.1.call-update) | async-done | bytes 2097168 | tf_op jit(solution)/shard_map/all_gather | solution.py:85
  35.8 372.3 %while.16 = (s32[]{:T(128)}, bf16[64,1024]{1,0:T(8,128)(2,1)S(1)}, bf16[64,1024]{1,0:T(8,128)(2,1)}, s32[]{:T(128)}, pred[]{:T(512)}, /*index=5*/bf16[1024,1024]...) while((s32[]{:T(128)}, bf16[64,1024]{1,0:T(8,128)(2,1)S(1)}, ...), condition=%wide.region_12.13_spmd, body=%wide.region_0.12_spmd.sunk | while | flops 812734080 | bytes 22180840 | solution.py:124
  39.9 13.1 %conditional.2 = (bf16[64,1024]{1,0:T(8,128)(2,1)S(1)}, f32[4,1024]{1,0:T(4,128)S(1)}) conditional(s32[]{:T(128)} %convert_element_type.185, bf16[64,1024]{1,0:T(8,128)(2,1)S(1)} %dynamic-slice_select_fusion.2, (bf16[64,1024]{1,0:T(8,128)(2,1)S(1)}, f32[2,1024]{1,0:T(2,128)}, bf16[1024,1536]{1,0:T(8,128)(2,1)}, bf16[512,1024]{1,0:T(8,128)(2,1)}, ...), branch_computations={%region_1.0_spmd, %region_3.11_spmd} | conditional | flops 812660352 | bytes 21230124 | solution.py:110
  47.7 5.3 convert_reduce_fusion.2
  57.5 13.1 %conditional.2 = (bf16[64,1024]{1,0:T(8,128)(2,1)S(1)}, f32[4,1024]{1,0:T(4,128)S(1)}) conditional(s32[]{:T(128)} %convert_element_type.185, bf16[64,1024]{1,0:T(8,128)(2,1)S(1)} %dynamic-slice_select_fusion.2, (bf16[64,1024]{1,0:T(8,128)(2,1)S(1)}, f32[2,1024]{1,0:T(2,128)}, bf16[1024,1536]{1,0:T(8,128)(2,1)}, bf16[512,1024]{1,0:T(8,128)(2,1)}, ...), branch_computations={%region_1.0_spmd, %region_3.11_spmd} | conditional | flops 812660352 | bytes 21230124 | solution.py:110
  65.3 5.3 convert_reduce_fusion.2
  76.1 13.1 %conditional.2 = (bf16[64,1024]{1,0:T(8,128)(2,1)S(1)}, f32[4,1024]{1,0:T(4,128)S(1)}) conditional(s32[]{:T(128)} %convert_element_type.185, bf16[64,1024]{1,0:T(8,128)(2,1)S(1)} %dynamic-slice_select_fusion.2, (bf16[64,1024]{1,0:T(8,128)(2,1)S(1)}, f32[2,1024]{1,0:T(2,128)}, bf16[1024,1536]{1,0:T(8,128)(2,1)}, bf16[512,1024]{1,0:T(8,128)(2,1)}, ...), branch_computations={%region_1.0_spmd, %region_3.11_spmd} | conditional | flops 812660352 | bytes 21230124 | solution.py:110
  83.9 5.3 convert_reduce_fusion.2
  95.2 13.1 %conditional.2 = (bf16[64,1024]{1,0:T(8,128)(2,1)S(1)}, f32[4,1024]{1,0:T(4,128)S(1)}) conditional(s32[]{:T(128)} %convert_element_type.185, bf16[64,1024]{1,0:T(8,128)(2,1)S(1)} %dynamic-slice_select_fusion.2, (bf16[64,1024]{1,0:T(8,128)(2,1)S(1)}, f32[2,1024]{1,0:T(2,128)}, bf16[1024,1536]{1,0:T(8,128)(2,1)}, bf16[512,1024]{1,0:T(8,128)(2,1)}, ...), branch_computations={%region_1.0_spmd, %region_3.11_spmd} | conditional | flops 812660352 | bytes 21230124 | solution.py:110
  103.0 5.3 convert_reduce_fusion.2
  109.7 5.3 %collective-permute-start = (bf16[64,1024]{1,0:T(8,128)(2,1)S(1)}, bf16[64,1024]{1,0:T(8,128)(2,1)S(1)}, u32[]{:S(2)}, u32[]{:S(2)}) collective-permute-start(bf16[64,1024]{1,0:T(8,128)(2,1)S(1)} %get-tuple-element.386), channel_id=1, source_target_pairs={{0,4},{4,8},{8,12},{1,5},{5,9},{9,13},{2,6},{6,10},{10,14},{3,7},{... | collective-permute-start | bytes 393224 | tf_op jit(solution)/shard_map/while/body/eval_jaxpr/ppermute | solution.py:16
  116.9 13.1 %conditional.2 = (bf16[64,1024]{1,0:T(8,128)(2,1)S(1)}, f32[4,1024]{1,0:T(4,128)S(1)}) conditional(s32[]{:T(128)} %convert_element_type.185, bf16[64,1024]{1,0:T(8,128)(2,1)S(1)} %dynamic-slice_select_fusion.2, (bf16[64,1024]{1,0:T(8,128)(2,1)S(1)}, f32[2,1024]{1,0:T(2,128)}, bf16[1024,1536]{1,0:T(8,128)(2,1)}, bf16[512,1024]{1,0:T(8,128)(2,1)}, ...), branch_computations={%region_1.0_spmd, %region_3.11_spmd} | conditional | flops 812660352 | bytes 21230124 | solution.py:110
  124.7 5.3 convert_reduce_fusion.2
  131.3 5.3 %collective-permute-start = (bf16[64,1024]{1,0:T(8,128)(2,1)S(1)}, bf16[64,1024]{1,0:T(8,128)(2,1)S(1)}, u32[]{:S(2)}, u32[]{:S(2)}) collective-permute-start(bf16[64,1024]{1,0:T(8,128)(2,1)S(1)} %get-tuple-element.386), channel_id=1, source_target_pairs={{0,4},{4,8},{8,12},{1,5},{5,9},{9,13},{2,6},{6,10},{10,14},{3,7},{... | collective-permute-start | bytes 393224 | tf_op jit(solution)/shard_map/while/body/eval_jaxpr/ppermute | solution.py:16
  138.5 13.1 %conditional.2 = (bf16[64,1024]{1,0:T(8,128)(2,1)S(1)}, f32[4,1024]{1,0:T(4,128)S(1)}) conditional(s32[]{:T(128)} %convert_element_type.185, bf16[64,1024]{1,0:T(8,128)(2,1)S(1)} %dynamic-slice_select_fusion.2, (bf16[64,1024]{1,0:T(8,128)(2,1)S(1)}, f32[2,1024]{1,0:T(2,128)}, bf16[1024,1536]{1,0:T(8,128)(2,1)}, bf16[512,1024]{1,0:T(8,128)(2,1)}, ...), branch_computations={%region_1.0_spmd, %region_3.11_spmd} | conditional | flops 812660352 | bytes 21230124 | solution.py:110
  152.9 5.3 %collective-permute-start = (bf16[64,1024]{1,0:T(8,128)(2,1)S(1)}, bf16[64,1024]{1,0:T(8,128)(2,1)S(1)}, u32[]{:S(2)}, u32[]{:S(2)}) collective-permute-start(bf16[64,1024]{1,0:T(8,128)(2,1)S(1)} %get-tuple-element.386), channel_id=1, source_target_pairs={{0,4},{4,8},{8,12},{1,5},{5,9},{9,13},{2,6},{6,10},{10,14},{3,7},{... | collective-permute-start | bytes 393224 | tf_op jit(solution)/shard_map/while/body/eval_jaxpr/ppermute | solution.py:16
  160.1 13.1 %conditional.2 = (bf16[64,1024]{1,0:T(8,128)(2,1)S(1)}, f32[4,1024]{1,0:T(4,128)S(1)}) conditional(s32[]{:T(128)} %convert_element_type.185, bf16[64,1024]{1,0:T(8,128)(2,1)S(1)} %dynamic-slice_select_fusion.2, (bf16[64,1024]{1,0:T(8,128)(2,1)S(1)}, f32[2,1024]{1,0:T(2,128)}, bf16[1024,1536]{1,0:T(8,128)(2,1)}, bf16[512,1024]{1,0:T(8,128)(2,1)}, ...), branch_computations={%region_1.0_spmd, %region_3.11_spmd} | conditional | flops 812660352 | bytes 21230124 | solution.py:110
  167.9 5.3 convert_reduce_fusion.2
  174.5 5.3 %collective-permute-start = (bf16[64,1024]{1,0:T(8,128)(2,1)S(1)}, bf16[64,1024]{1,0:T(8,128)(2,1)S(1)}, u32[]{:S(2)}, u32[]{:S(2)}) collective-permute-start(bf16[64,1024]{1,0:T(8,128)(2,1)S(1)} %get-tuple-element.386), channel_id=1, source_target_pairs={{0,4},{4,8},{8,12},{1,5},{5,9},{9,13},{2,6},{6,10},{10,14},{3,7},{... | collective-permute-start | bytes 393224 | tf_op jit(solution)/shard_map/while/body/eval_jaxpr/ppermute | solution.py:16
  181.8 13.1 %conditional.2 = (bf16[64,1024]{1,0:T(8,128)(2,1)S(1)}, f32[4,1024]{1,0:T(4,128)S(1)}) conditional(s32[]{:T(128)} %convert_element_type.185, bf16[64,1024]{1,0:T(8,128)(2,1)S(1)} %dynamic-slice_select_fusion.2, (bf16[64,1024]{1,0:T(8,128)(2,1)S(1)}, f32[2,1024]{1,0:T(2,128)}, bf16[1024,1536]{1,0:T(8,128)(2,1)}, bf16[512,1024]{1,0:T(8,128)(2,1)}, ...), branch_computations={%region_1.0_spmd, %region_3.11_spmd} | conditional | flops 812660352 | bytes 21230124 | solution.py:110
  196.2 5.3 %collective-permute-start = (bf16[64,1024]{1,0:T(8,128)(2,1)S(1)}, bf16[64,1024]{1,0:T(8,128)(2,1)S(1)}, u32[]{:S(2)}, u32[]{:S(2)}) collective-permute-start(bf16[64,1024]{1,0:T(8,128)(2,1)S(1)} %get-tuple-element.386), channel_id=1, source_target_pairs={{0,4},{4,8},{8,12},{1,5},{5,9},{9,13},{2,6},{6,10},{10,14},{3,7},{... | collective-permute-start | bytes 393224 | tf_op jit(solution)/shard_map/while/body/eval_jaxpr/ppermute | solution.py:16
  203.4 13.1 %conditional.2 = (bf16[64,1024]{1,0:T(8,128)(2,1)S(1)}, f32[4,1024]{1,0:T(4,128)S(1)}) conditional(s32[]{:T(128)} %convert_element_type.185, bf16[64,1024]{1,0:T(8,128)(2,1)S(1)} %dynamic-slice_select_fusion.2, (bf16[64,1024]{1,0:T(8,128)(2,1)S(1)}, f32[2,1024]{1,0:T(2,128)}, bf16[1024,1536]{1,0:T(8,128)(2,1)}, bf16[512,1024]{1,0:T(8,128)(2,1)}, ...), branch_computations={%region_1.0_spmd, %region_3.11_spmd} | conditional | flops 812660352 | bytes 21230124 | solution.py:110
  211.2 5.3 convert_reduce_fusion.2
  217.8 5.3 %collective-permute-start = (bf16[64,1024]{1,0:T(8,128)(2,1)S(1)}, bf16[64,1024]{1,0:T(8,128)(2,1)S(1)}, u32[]{:S(2)}, u32[]{:S(2)}) collective-permute-start(bf16[64,1024]{1,0:T(8,128)(2,1)S(1)} %get-tuple-element.386), channel_id=1, source_target_pairs={{0,4},{4,8},{8,12},{1,5},{5,9},{9,13},{2,6},{6,10},{10,14},{3,7},{... | collective-permute-start | bytes 393224 | tf_op jit(solution)/shard_map/while/body/eval_jaxpr/ppermute | solution.py:16
  225.0 13.1 %conditional.2 = (bf16[64,1024]{1,0:T(8,128)(2,1)S(1)}, f32[4,1024]{1,0:T(4,128)S(1)}) conditional(s32[]{:T(128)} %convert_element_type.185, bf16[64,1024]{1,0:T(8,128)(2,1)S(1)} %dynamic-slice_select_fusion.2, (bf16[64,1024]{1,0:T(8,128)(2,1)S(1)}, f32[2,1024]{1,0:T(2,128)}, bf16[1024,1536]{1,0:T(8,128)(2,1)}, bf16[512,1024]{1,0:T(8,128)(2,1)}, ...), branch_computations={%region_1.0_spmd, %region_3.11_spmd} | conditional | flops 812660352 | bytes 21230124 | solution.py:110
  232.8 5.3 convert_reduce_fusion.2
  239.4 5.3 %collective-permute-start = (bf16[64,1024]{1,0:T(8,128)(2,1)S(1)}, bf16[64,1024]{1,0:T(8,128)(2,1)S(1)}, u32[]{:S(2)}, u32[]{:S(2)}) collective-permute-start(bf16[64,1024]{1,0:T(8,128)(2,1)S(1)} %get-tuple-element.386), channel_id=1, source_target_pairs={{0,4},{4,8},{8,12},{1,5},{5,9},{9,13},{2,6},{6,10},{10,14},{3,7},{... | collective-permute-start | bytes 393224 | tf_op jit(solution)/shard_map/while/body/eval_jaxpr/ppermute | solution.py:16
  246.6 13.1 %conditional.2 = (bf16[64,1024]{1,0:T(8,128)(2,1)S(1)}, f32[4,1024]{1,0:T(4,128)S(1)}) conditional(s32[]{:T(128)} %convert_element_type.185, bf16[64,1024]{1,0:T(8,128)(2,1)S(1)} %dynamic-slice_select_fusion.2, (bf16[64,1024]{1,0:T(8,128)(2,1)S(1)}, f32[2,1024]{1,0:T(2,128)}, bf16[1024,1536]{1,0:T(8,128)(2,1)}, bf16[512,1024]{1,0:T(8,128)(2,1)}, ...), branch_computations={%region_1.0_spmd, %region_3.11_spmd} | conditional | flops 812660352 | bytes 21230124 | solution.py:110
  254.4 5.3 convert_reduce_fusion.2
  261.0 5.3 %collective-permute-start = (bf16[64,1024]{1,0:T(8,128)(2,1)S(1)}, bf16[64,1024]{1,0:T(8,128)(2,1)S(1)}, u32[]{:S(2)}, u32[]{:S(2)}) collective-permute-start(bf16[64,1024]{1,0:T(8,128)(2,1)S(1)} %get-tuple-element.386), channel_id=1, source_target_pairs={{0,4},{4,8},{8,12},{1,5},{5,9},{9,13},{2,6},{6,10},{10,14},{3,7},{... | collective-permute-start | bytes 393224 | tf_op jit(solution)/shard_map/while/body/eval_jaxpr/ppermute | solution.py:16
  268.3 13.1 %conditional.2 = (bf16[64,1024]{1,0:T(8,128)(2,1)S(1)}, f32[4,1024]{1,0:T(4,128)S(1)}) conditional(s32[]{:T(128)} %convert_element_type.185, bf16[64,1024]{1,0:T(8,128)(2,1)S(1)} %dynamic-slice_select_fusion.2, (bf16[64,1024]{1,0:T(8,128)(2,1)S(1)}, f32[2,1024]{1,0:T(2,128)}, bf16[1024,1536]{1,0:T(8,128)(2,1)}, bf16[512,1024]{1,0:T(8,128)(2,1)}, ...), branch_computations={%region_1.0_spmd, %region_3.11_spmd} | conditional | flops 812660352 | bytes 21230124 | solution.py:110
  276.1 5.3 convert_reduce_fusion.2
  282.7 5.3 %collective-permute-start = (bf16[64,1024]{1,0:T(8,128)(2,1)S(1)}, bf16[64,1024]{1,0:T(8,128)(2,1)S(1)}, u32[]{:S(2)}, u32[]{:S(2)}) collective-permute-start(bf16[64,1024]{1,0:T(8,128)(2,1)S(1)} %get-tuple-element.386), channel_id=1, source_target_pairs={{0,4},{4,8},{8,12},{1,5},{5,9},{9,13},{2,6},{6,10},{10,14},{3,7},{... | collective-permute-start | bytes 393224 | tf_op jit(solution)/shard_map/while/body/eval_jaxpr/ppermute | solution.py:16
  289.9 13.1 %conditional.2 = (bf16[64,1024]{1,0:T(8,128)(2,1)S(1)}, f32[4,1024]{1,0:T(4,128)S(1)}) conditional(s32[]{:T(128)} %convert_element_type.185, bf16[64,1024]{1,0:T(8,128)(2,1)S(1)} %dynamic-slice_select_fusion.2, (bf16[64,1024]{1,0:T(8,128)(2,1)S(1)}, f32[2,1024]{1,0:T(2,128)}, bf16[1024,1536]{1,0:T(8,128)(2,1)}, bf16[512,1024]{1,0:T(8,128)(2,1)}, ...), branch_computations={%region_1.0_spmd, %region_3.11_spmd} | conditional | flops 812660352 | bytes 21230124 | solution.py:110
  304.3 5.3 %collective-permute-start = (bf16[64,1024]{1,0:T(8,128)(2,1)S(1)}, bf16[64,1024]{1,0:T(8,128)(2,1)S(1)}, u32[]{:S(2)}, u32[]{:S(2)}) collective-permute-start(bf16[64,1024]{1,0:T(8,128)(2,1)S(1)} %get-tuple-element.386), channel_id=1, source_target_pairs={{0,4},{4,8},{8,12},{1,5},{5,9},{9,13},{2,6},{6,10},{10,14},{3,7},{... | collective-permute-start | bytes 393224 | tf_op jit(solution)/shard_map/while/body/eval_jaxpr/ppermute | solution.py:16
  311.5 13.1 %conditional.2 = (bf16[64,1024]{1,0:T(8,128)(2,1)S(1)}, f32[4,1024]{1,0:T(4,128)S(1)}) conditional(s32[]{:T(128)} %convert_element_type.185, bf16[64,1024]{1,0:T(8,128)(2,1)S(1)} %dynamic-slice_select_fusion.2, (bf16[64,1024]{1,0:T(8,128)(2,1)S(1)}, f32[2,1024]{1,0:T(2,128)}, bf16[1024,1536]{1,0:T(8,128)(2,1)}, bf16[512,1024]{1,0:T(8,128)(2,1)}, ...), branch_computations={%region_1.0_spmd, %region_3.11_spmd} | conditional | flops 812660352 | bytes 21230124 | solution.py:110
  325.9 5.3 %collective-permute-start = (bf16[64,1024]{1,0:T(8,128)(2,1)S(1)}, bf16[64,1024]{1,0:T(8,128)(2,1)S(1)}, u32[]{:S(2)}, u32[]{:S(2)}) collective-permute-start(bf16[64,1024]{1,0:T(8,128)(2,1)S(1)} %get-tuple-element.386), channel_id=1, source_target_pairs={{0,4},{4,8},{8,12},{1,5},{5,9},{9,13},{2,6},{6,10},{10,14},{3,7},{... | collective-permute-start | bytes 393224 | tf_op jit(solution)/shard_map/while/body/eval_jaxpr/ppermute | solution.py:16
  333.1 13.1 %conditional.2 = (bf16[64,1024]{1,0:T(8,128)(2,1)S(1)}, f32[4,1024]{1,0:T(4,128)S(1)}) conditional(s32[]{:T(128)} %convert_element_type.185, bf16[64,1024]{1,0:T(8,128)(2,1)S(1)} %dynamic-slice_select_fusion.2, (bf16[64,1024]{1,0:T(8,128)(2,1)S(1)}, f32[2,1024]{1,0:T(2,128)}, bf16[1024,1536]{1,0:T(8,128)(2,1)}, bf16[512,1024]{1,0:T(8,128)(2,1)}, ...), branch_computations={%region_1.0_spmd, %region_3.11_spmd} | conditional | flops 812660352 | bytes 21230124 | solution.py:110
  347.5 5.3 %collective-permute-start = (bf16[64,1024]{1,0:T(8,128)(2,1)S(1)}, bf16[64,1024]{1,0:T(8,128)(2,1)S(1)}, u32[]{:S(2)}, u32[]{:S(2)}) collective-permute-start(bf16[64,1024]{1,0:T(8,128)(2,1)S(1)} %get-tuple-element.386), channel_id=1, source_target_pairs={{0,4},{4,8},{8,12},{1,5},{5,9},{9,13},{2,6},{6,10},{10,14},{3,7},{... | collective-permute-start | bytes 393224 | tf_op jit(solution)/shard_map/while/body/eval_jaxpr/ppermute | solution.py:16
  354.8 13.1 %conditional.2 = (bf16[64,1024]{1,0:T(8,128)(2,1)S(1)}, f32[4,1024]{1,0:T(4,128)S(1)}) conditional(s32[]{:T(128)} %convert_element_type.185, bf16[64,1024]{1,0:T(8,128)(2,1)S(1)} %dynamic-slice_select_fusion.2, (bf16[64,1024]{1,0:T(8,128)(2,1)S(1)}, f32[2,1024]{1,0:T(2,128)}, bf16[1024,1536]{1,0:T(8,128)(2,1)}, bf16[512,1024]{1,0:T(8,128)(2,1)}, ...), branch_computations={%region_1.0_spmd, %region_3.11_spmd} | conditional | flops 812660352 | bytes 21230124 | solution.py:110
  369.2 5.3 %collective-permute-start = (bf16[64,1024]{1,0:T(8,128)(2,1)S(1)}, bf16[64,1024]{1,0:T(8,128)(2,1)S(1)}, u32[]{:S(2)}, u32[]{:S(2)}) collective-permute-start(bf16[64,1024]{1,0:T(8,128)(2,1)S(1)} %get-tuple-element.386), channel_id=1, source_target_pairs={{0,4},{4,8},{8,12},{1,5},{5,9},{9,13},{2,6},{6,10},{10,14},{3,7},{... | collective-permute-start | bytes 393224 | tf_op jit(solution)/shard_map/while/body/eval_jaxpr/ppermute | solution.py:16
  377.8 18.3 %collective-permute-start = (bf16[64,1024]{1,0:T(8,128)(2,1)S(1)}, bf16[64,1024]{1,0:T(8,128)(2,1)S(1)}, u32[]{:S(2)}, u32[]{:S(2)}) collective-permute-start(bf16[64,1024]{1,0:T(8,128)(2,1)S(1)} %get-tuple-element.386), channel_id=1, source_target_pairs={{0,4},{4,8},{8,12},{1,5},{5,9},{9,13},{2,6},{6,10},{10,14},{3,7},{... | collective-permute-start | bytes 393224 | tf_op jit(solution)/shard_map/while/body/eval_jaxpr/ppermute | solution.py:16
  399.4 5.3 %collective-permute-start = (bf16[64,1024]{1,0:T(8,128)(2,1)S(1)}, bf16[64,1024]{1,0:T(8,128)(2,1)S(1)}, u32[]{:S(2)}, u32[]{:S(2)}) collective-permute-start(bf16[64,1024]{1,0:T(8,128)(2,1)S(1)} %get-tuple-element.386), channel_id=1, source_target_pairs={{0,4},{4,8},{8,12},{1,5},{5,9},{9,13},{2,6},{6,10},{10,14},{3,7},{... | collective-permute-start | bytes 393224 | tf_op jit(solution)/shard_map/while/body/eval_jaxpr/ppermute | solution.py:16
  408.1 34.8 %all-gather = bf16[256,1024]{1,0:T(8,128)(2,1)S(1)} all-gather(bf16[64,1024]{1,0:T(8,128)(2,1)S(1)} %convert_select_fusion), channel_id=2, replica_groups=mesh['groups'=2,'section'=4,'dp'=4] {'section'}, dimensions={0}, use_global_device_ids=true | all-gather | bytes 655360 | tf_op jit(solution)/shard_map/all_gather | solution.py:21
  443.0 16.2 %all_gather.15 = bf16[256,1024]{1,0:T(8,128)(2,1)S(1)} all-gather(bf16[64,1024]{1,0:T(8,128)(2,1)S(1)} %reduce_sum.96), channel_id=1, replica_groups=mesh['groups'=2,'section'=4,'dp'=4] {'dp'}, dimensions={0}, use_global_device_ids=true | all-gather | bytes 655360 | tf_op jit(solution)/shard_map/all_gather | solution.py:136
  466.3 31.3 %all-reduce.3.cloned.1.call-done = bf16[33,1024]{1,0:T(8,128)(2,1)} async-done(((bf16[33,1024]{1,0:T(8,128)(2,1)}), bf16[33,1024]{1,0:T(8,128)(2,1)}) %all-reduce.3.cloned.1.call-update) | async-done | bytes 67600 | tf_op jit(solution)/shard_map/psum | solution.py:148
  498.9 10.7 %psum.30 = bf16[16,1024]{1,0:T(8,128)(2,1)S(1)} all-reduce(bf16[16,1024]{1,0:T(8,128)(2,1)S(1)} %convolution_convert_fusion.2), channel_id=1, replica_groups=mesh['groups'=2,'section'=4,'dp'=4] {'section'}, use_global_device_ids=true, to_apply=%region_16.17 | all-reduce | flops 16384 | bytes 65536 | tf_op jit(solution)/shard_map/psum | solution.py:153
  509.8 11.1 %all-reduce = (f32[32,22]{0,1:T(8,128)}, f32[16,22]{1,0:T(8,128)}) all-reduce(f32[32,22]{0,1:T(8,128)S(1)} %fusion.70, f32[16,22]{1,0:T(8,128)S(1)} %fusion.72), channel_id=1, replica_groups=mesh['groups'=2,'section'=4,'dp'=4] {'section'}, use_global_device_ids=true, to_apply=%region_15.16 | all-reduce | flops 1056 | bytes 8448 | tf_op jit(solution)/shard_map/psum | solution.py:158
  (460 shorter events, 236.4 us)
Async XLA Ops:
  7.2 458.1 %copy-start = (bf16[3,256,1024]{2,1,0:T(8,128)(2,1)S(1)}, bf16[3,256,1024]{2,1,0:T(8,128)(2,1)}, u32[]{:S(2)}) copy-start(bf16[3,256,1024]{2,1,0:T(8,128)(2,1)} %param.21) | copy-start | bytes 4718596
  7.2 27.9 %all-gather.3.cloned.1.call-start = ((), (), s32[]{:S(2)}) async-start(), calls=%async_computation | async-start | bytes 2621440 | tf_op jit(solution)/shard_map/all_gather | solution.py:85
  7.9 489.8 %all-reduce.3.cloned.1.call-start = ((), (), s32[]{:S(2)}) async-start(), calls=%async_computation.1 | async-start | bytes 163840 | tf_op jit(solution)/shard_map/psum | solution.py:148
  35.8 3.1 collective-permute-start
  44.4 2.7 copy-start.1
  54.3 2.3 collective-permute-start
  62.0 2.7 copy-start.1
  71.9 3.2 collective-permute-start
  80.6 2.7 copy-start.1
  90.5 3.8 collective-permute-start
  99.8 2.7 copy-start.1
  109.7 6.3 %collective-permute-start = (bf16[64,1024]{1,0:T(8,128)(2,1)S(1)}, bf16[64,1024]{1,0:T(8,128)(2,1)S(1)}, u32[]{:S(2)}, u32[]{:S(2)}) collective-permute-start(bf16[64,1024]{1,0:T(8,128)(2,1)S(1)} %get-tuple-element.386), channel_id=1, source_target_pairs={{0,4},{4,8},{8,12},{1,5},{5,9},{9,13},{2,6},{6,10},{10,14},{3,7},{... | collective-permute-start | bytes 393224 | tf_op jit(solution)/shard_map/while/body/eval_jaxpr/ppermute | solution.py:16
  121.4 2.7 copy-start.1
  131.3 6.3 %collective-permute-start = (bf16[64,1024]{1,0:T(8,128)(2,1)S(1)}, bf16[64,1024]{1,0:T(8,128)(2,1)S(1)}, u32[]{:S(2)}, u32[]{:S(2)}) collective-permute-start(bf16[64,1024]{1,0:T(8,128)(2,1)S(1)} %get-tuple-element.386), channel_id=1, source_target_pairs={{0,4},{4,8},{8,12},{1,5},{5,9},{9,13},{2,6},{6,10},{10,14},{3,7},{... | collective-permute-start | bytes 393224 | tf_op jit(solution)/shard_map/while/body/eval_jaxpr/ppermute | solution.py:16
  143.0 2.7 copy-start.1
  152.9 6.3 %collective-permute-start = (bf16[64,1024]{1,0:T(8,128)(2,1)S(1)}, bf16[64,1024]{1,0:T(8,128)(2,1)S(1)}, u32[]{:S(2)}, u32[]{:S(2)}) collective-permute-start(bf16[64,1024]{1,0:T(8,128)(2,1)S(1)} %get-tuple-element.386), channel_id=1, source_target_pairs={{0,4},{4,8},{8,12},{1,5},{5,9},{9,13},{2,6},{6,10},{10,14},{3,7},{... | collective-permute-start | bytes 393224 | tf_op jit(solution)/shard_map/while/body/eval_jaxpr/ppermute | solution.py:16
  164.6 2.7 copy-start.1
  174.5 6.3 %collective-permute-start = (bf16[64,1024]{1,0:T(8,128)(2,1)S(1)}, bf16[64,1024]{1,0:T(8,128)(2,1)S(1)}, u32[]{:S(2)}, u32[]{:S(2)}) collective-permute-start(bf16[64,1024]{1,0:T(8,128)(2,1)S(1)} %get-tuple-element.386), channel_id=1, source_target_pairs={{0,4},{4,8},{8,12},{1,5},{5,9},{9,13},{2,6},{6,10},{10,14},{3,7},{... | collective-permute-start | bytes 393224 | tf_op jit(solution)/shard_map/while/body/eval_jaxpr/ppermute | solution.py:16
  186.3 2.7 copy-start.1
  196.2 6.3 %collective-permute-start = (bf16[64,1024]{1,0:T(8,128)(2,1)S(1)}, bf16[64,1024]{1,0:T(8,128)(2,1)S(1)}, u32[]{:S(2)}, u32[]{:S(2)}) collective-permute-start(bf16[64,1024]{1,0:T(8,128)(2,1)S(1)} %get-tuple-element.386), channel_id=1, source_target_pairs={{0,4},{4,8},{8,12},{1,5},{5,9},{9,13},{2,6},{6,10},{10,14},{3,7},{... | collective-permute-start | bytes 393224 | tf_op jit(solution)/shard_map/while/body/eval_jaxpr/ppermute | solution.py:16
  207.9 2.7 copy-start.1
  217.8 6.3 %collective-permute-start = (bf16[64,1024]{1,0:T(8,128)(2,1)S(1)}, bf16[64,1024]{1,0:T(8,128)(2,1)S(1)}, u32[]{:S(2)}, u32[]{:S(2)}) collective-permute-start(bf16[64,1024]{1,0:T(8,128)(2,1)S(1)} %get-tuple-element.386), channel_id=1, source_target_pairs={{0,4},{4,8},{8,12},{1,5},{5,9},{9,13},{2,6},{6,10},{10,14},{3,7},{... | collective-permute-start | bytes 393224 | tf_op jit(solution)/shard_map/while/body/eval_jaxpr/ppermute | solution.py:16
  229.5 2.7 copy-start.1
  239.4 6.3 %collective-permute-start = (bf16[64,1024]{1,0:T(8,128)(2,1)S(1)}, bf16[64,1024]{1,0:T(8,128)(2,1)S(1)}, u32[]{:S(2)}, u32[]{:S(2)}) collective-permute-start(bf16[64,1024]{1,0:T(8,128)(2,1)S(1)} %get-tuple-element.386), channel_id=1, source_target_pairs={{0,4},{4,8},{8,12},{1,5},{5,9},{9,13},{2,6},{6,10},{10,14},{3,7},{... | collective-permute-start | bytes 393224 | tf_op jit(solution)/shard_map/while/body/eval_jaxpr/ppermute | solution.py:16
  251.2 2.7 copy-start.1
  261.0 6.3 %collective-permute-start = (bf16[64,1024]{1,0:T(8,128)(2,1)S(1)}, bf16[64,1024]{1,0:T(8,128)(2,1)S(1)}, u32[]{:S(2)}, u32[]{:S(2)}) collective-permute-start(bf16[64,1024]{1,0:T(8,128)(2,1)S(1)} %get-tuple-element.386), channel_id=1, source_target_pairs={{0,4},{4,8},{8,12},{1,5},{5,9},{9,13},{2,6},{6,10},{10,14},{3,7},{... | collective-permute-start | bytes 393224 | tf_op jit(solution)/shard_map/while/body/eval_jaxpr/ppermute | solution.py:16
  272.8 2.7 copy-start.1
  282.7 6.3 %collective-permute-start = (bf16[64,1024]{1,0:T(8,128)(2,1)S(1)}, bf16[64,1024]{1,0:T(8,128)(2,1)S(1)}, u32[]{:S(2)}, u32[]{:S(2)}) collective-permute-start(bf16[64,1024]{1,0:T(8,128)(2,1)S(1)} %get-tuple-element.386), channel_id=1, source_target_pairs={{0,4},{4,8},{8,12},{1,5},{5,9},{9,13},{2,6},{6,10},{10,14},{3,7},{... | collective-permute-start | bytes 393224 | tf_op jit(solution)/shard_map/while/body/eval_jaxpr/ppermute | solution.py:16
  294.4 2.7 copy-start.1
  304.3 6.3 %collective-permute-start = (bf16[64,1024]{1,0:T(8,128)(2,1)S(1)}, bf16[64,1024]{1,0:T(8,128)(2,1)S(1)}, u32[]{:S(2)}, u32[]{:S(2)}) collective-permute-start(bf16[64,1024]{1,0:T(8,128)(2,1)S(1)} %get-tuple-element.386), channel_id=1, source_target_pairs={{0,4},{4,8},{8,12},{1,5},{5,9},{9,13},{2,6},{6,10},{10,14},{3,7},{... | collective-permute-start | bytes 393224 | tf_op jit(solution)/shard_map/while/body/eval_jaxpr/ppermute | solution.py:16
  316.0 2.7 copy-start.1
  325.9 6.3 %collective-permute-start = (bf16[64,1024]{1,0:T(8,128)(2,1)S(1)}, bf16[64,1024]{1,0:T(8,128)(2,1)S(1)}, u32[]{:S(2)}, u32[]{:S(2)}) collective-permute-start(bf16[64,1024]{1,0:T(8,128)(2,1)S(1)} %get-tuple-element.386), channel_id=1, source_target_pairs={{0,4},{4,8},{8,12},{1,5},{5,9},{9,13},{2,6},{6,10},{10,14},{3,7},{... | collective-permute-start | bytes 393224 | tf_op jit(solution)/shard_map/while/body/eval_jaxpr/ppermute | solution.py:16
  337.7 2.7 copy-start.1
  347.5 6.3 %collective-permute-start = (bf16[64,1024]{1,0:T(8,128)(2,1)S(1)}, bf16[64,1024]{1,0:T(8,128)(2,1)S(1)}, u32[]{:S(2)}, u32[]{:S(2)}) collective-permute-start(bf16[64,1024]{1,0:T(8,128)(2,1)S(1)} %get-tuple-element.386), channel_id=1, source_target_pairs={{0,4},{4,8},{8,12},{1,5},{5,9},{9,13},{2,6},{6,10},{10,14},{3,7},{... | collective-permute-start | bytes 393224 | tf_op jit(solution)/shard_map/while/body/eval_jaxpr/ppermute | solution.py:16
  359.3 2.7 copy-start.1
  369.2 6.3 %collective-permute-start = (bf16[64,1024]{1,0:T(8,128)(2,1)S(1)}, bf16[64,1024]{1,0:T(8,128)(2,1)S(1)}, u32[]{:S(2)}, u32[]{:S(2)}) collective-permute-start(bf16[64,1024]{1,0:T(8,128)(2,1)S(1)} %get-tuple-element.386), channel_id=1, source_target_pairs={{0,4},{4,8},{8,12},{1,5},{5,9},{9,13},{2,6},{6,10},{10,14},{3,7},{... | collective-permute-start | bytes 393224 | tf_op jit(solution)/shard_map/while/body/eval_jaxpr/ppermute | solution.py:16
  377.8 19.3 %collective-permute-start = (bf16[64,1024]{1,0:T(8,128)(2,1)S(1)}, bf16[64,1024]{1,0:T(8,128)(2,1)S(1)}, u32[]{:S(2)}, u32[]{:S(2)}) collective-permute-start(bf16[64,1024]{1,0:T(8,128)(2,1)S(1)} %get-tuple-element.386), channel_id=1, source_target_pairs={{0,4},{4,8},{8,12},{1,5},{5,9},{9,13},{2,6},{6,10},{10,14},{3,7},{... | collective-permute-start | bytes 393224 | tf_op jit(solution)/shard_map/while/body/eval_jaxpr/ppermute | solution.py:16
  399.4 6.3 %collective-permute-start = (bf16[64,1024]{1,0:T(8,128)(2,1)S(1)}, bf16[64,1024]{1,0:T(8,128)(2,1)S(1)}, u32[]{:S(2)}, u32[]{:S(2)}) collective-permute-start(bf16[64,1024]{1,0:T(8,128)(2,1)S(1)} %get-tuple-element.386), channel_id=1, source_target_pairs={{0,4},{4,8},{8,12},{1,5},{5,9},{9,13},{2,6},{6,10},{10,14},{3,7},{... | collective-permute-start | bytes 393224 | tf_op jit(solution)/shard_map/while/body/eval_jaxpr/ppermute | solution.py:16
  408.0 90.4 %copy-start.3 = (bf16[256,22]{0,1:T(8,128)(2,1)S(1)}, bf16[256,22]{0,1:T(8,128)(2,1)}, u32[]{:S(2)}) copy-start(bf16[256,22]{0,1:T(8,128)(2,1)} %param.23) | copy-start | bytes 33796
  443.0 55.7 %copy-start.2 = (bf16[3,256,1024]{2,1,0:T(8,128)(2,1)S(1)}, bf16[3,256,1024]{2,1,0:T(8,128)(2,1)}, u32[]{:S(2)}) copy-start(bf16[3,256,1024]{2,1,0:T(8,128)(2,1)} %param.22) | copy-start | bytes 4718596
  460.1 5.1 collective-permute-start.1
Sparse Core Ops, SparseCore 0:
  9.5 25.5 all-gather.2
  466.5 31.1 all-reduce.2
